TPU v7x, 32 devices: a whole 2x2x4 slice. The times are simulated.
32 devices in a mesh: wa: 16 (over z, y, core), gy: 2 (over x).
Axes of the slice: x: 2, y: 2, z: 4, core: 2. Of those that a mesh axis runs over, the one named last changes fastest.
Arguments:
- input_moments: float32 [120, 128, 32], P(None, 'wa', 'gy'), may hold values from -6 to 6
- solid_cell_mask: int32 [128, 32], P('wa', 'gy'), may hold values 0 or 1
- collision_coefficients: float32 [120, 120], replicated, may hold values from -0.5 to 0.5
- relaxation_rates: float32 [120], replicated, may hold values from 0.1 to 1
Outputs:
- final_state: float32 [120, 128, 32], P(None, 'wa', 'gy')
All inputs are finite; a program needn't handle non-finite values. No bound on the sum of `solid_cell_mask` on one device may be relied on, other than what follows from the above.
Results may differ from a plain program's by a relative error of at most 0.0003.
Values sent between devices are 32-bit elements; how exact they have to be, the bound alone decides.
No kernel may reach another device: no remote copies, remote signals or barrier semaphores. Data moves between devices by JAX's collectives and lax.ppermute only.
A program may use at most 64 MiB of HBM per device.

v0:
```python
import math
import jax
import jax.numpy as jnp
import numpy as np
from jax import lax
from jax.sharding import PartitionSpec as P

DEG = 7
ITERS = 2
highest_degree = lax.Precision.HIGHEST
axial_step = 0.2
cross_step = 0.2
collide_step = 0.5


def shifted(value, axis, by):
    count = lax.axis_size(axis)
    return lax.ppermute(value, axis, [(i, (i + by) % count) for i in range(count)])


def from_behind(value, axis, by):
    count = lax.axis_size(axis)
    pairs = [(i, i + by) for i in range(count) if 0 <= i + by < count]
    return lax.ppermute(value, axis, pairs)


def moment_table():
    entries = []
    for degree_now in range(DEG + 1):
        for first_k in range(degree_now, -1, -1):
            for second_k in range(degree_now - first_k, -1, -1):
                entries.append((first_k, second_k, degree_now - first_k - second_k))
    return entries


def hermite_value(order, point):
    previous = 1.0
    current_moments = point
    for level in range(1, order):
        previous, current_moments = (current_moments, point * current_moments - level * previous)
    return current_moments


def largest_root(order):
    upper = 2.0 * math.sqrt(order) + 1.0
    value_high = hermite_value(order, upper)
    lower = upper
    for trial in range(100000):
        lower = lower - 0.001
        value_low = hermite_value(order, lower)
        if (value_low > 0.0) != (value_high > 0.0):
            break
        upper = lower
        value_high = value_low
    for repeat in range(80):
        middle = 0.5 * (lower + upper)
        value_mid = hermite_value(order, middle)
        if (value_mid > 0.0) == (value_high > 0.0):
            upper = middle
            value_high = value_mid
        else:
            lower = middle
    return 0.5 * (lower + upper)


def coupling(entries, lookup, direction):
    matrix = np.zeros((len(entries), len(entries)), dtype=np.float32)
    for position, moment in enumerate(entries):
        raised = list(moment)
        raised[direction] += 1
        raised = tuple(raised)
        if raised in lookup:
            partner = lookup[raised]
            matrix[position, partner] = math.sqrt(moment[direction] + 1)
            matrix[partner, position] = math.sqrt(moment[direction] + 1)
    return matrix


def to_float(table):
    return jnp.asarray(table, dtype=jnp.float32)


def operator_tables():
    entries = moment_table()
    number = len(entries)
    lookup = {moment: position for position, moment in enumerate(entries)}
    axial_matrix = coupling(entries, lookup, 0)
    cross_matrix = coupling(entries, lookup, 1)
    degrees = np.array([sum(moment) for moment in entries])
    degree_band_mask = (
        (np.abs(degrees[:, None] - degrees[None, :]) <= 1)
        & (degrees[:, None] >= 2)
        & (degrees[None, :] >= 2)
    ).astype(np.float32)
    unit_rows = [lookup[1, 0, 0], lookup[0, 1, 0], lookup[0, 0, 1]]
    first_selection = np.zeros((number, number), dtype=np.float32)
    second_selection = np.zeros((number, number), dtype=np.float32)
    moment_weights = np.zeros(number, dtype=np.float32)
    for position, moment in enumerate(entries):
        if sum(moment) == 2:
            raised = [direction for direction in range(3) for repeat in range(moment[direction])]
            first_selection[position, unit_rows[raised[0]]] = 1.0
            second_selection[position, unit_rows[raised[1]]] = 1.0
            moment_weights[position] = 1.0 / math.sqrt(2.0) if raised[0] == raised[1] else 1.0
    relaxed = (degrees >= 2).astype(np.float32)
    density = (degrees == 0).astype(np.float32)
    speed_bound = largest_root(DEG + 1)
    return (
        to_float(axial_matrix),
        to_float(cross_matrix),
        to_float(degree_band_mask),
        to_float(first_selection),
        to_float(second_selection),
        to_float(moment_weights),
        to_float(relaxed),
        to_float(density),
        speed_bound,
    )


def wave_numbers(length):
    position = jnp.arange(length, dtype=jnp.int32)
    signed = jnp.where(position < length // 2, position, position - length)
    return signed.astype(jnp.float32) * (axial_step * 2.0 * math.pi / length)


def fourier_tables(length):
    position = jnp.arange(length, dtype=jnp.int32)
    phase_index = position[:, None] * position[None, :] % length
    angles = phase_index.astype(jnp.float32) * (2.0 * math.pi / length)
    return (jnp.cos(angles), jnp.sin(angles))


def phase_series(real_part, imag_part, axial_matrix, wave_scale):
    total_real, total_imag = (real_part, imag_part)
    term_real, term_imag = (real_part, imag_part)
    for term_order in range(1, 5):
        pushed_real = (
            jnp.einsum("js,suv->juv", axial_matrix, term_real, precision=highest_degree)
            * wave_scale[None, :, None]
        )
        pushed_imag = (
            jnp.einsum("js,suv->juv", axial_matrix, term_imag, precision=highest_degree)
            * wave_scale[None, :, None]
        )
        term_real, term_imag = (pushed_imag / term_order, -pushed_real / term_order)
        total_real = total_real + term_real
        total_imag = total_imag + term_imag
    return (total_real, total_imag)


def axial_update(line_field, cosine_table, sine_table, axial_matrix, wave_scale):
    length = line_field.shape[1]
    real_part = jnp.einsum("mxl,xk->mkl", line_field, cosine_table, precision=highest_degree)
    imag_part = -jnp.einsum("mxl,xk->mkl", line_field, sine_table, precision=highest_degree)
    total_real, total_imag = phase_series(real_part, imag_part, axial_matrix, wave_scale)
    restored = jnp.einsum("mkl,kx->mxl", total_real, cosine_table, precision=highest_degree)
    restored = restored - jnp.einsum(
        "mkl,kx->mxl", total_imag, sine_table, precision=highest_degree
    )
    return restored / length


def cross_update(current_moments, lower_rim, upper_rim, cross_matrix, speed_bound):
    central = jnp.einsum(
        "js,suv->juv", cross_matrix, upper_rim - lower_rim, precision=highest_degree
    )
    return current_moments - cross_step * (
        0.5 * central - 0.5 * speed_bound * (upper_rim - 2.0 * current_moments + lower_rim)
    )


def apply_walls(current_moments, mask_float, density):
    return current_moments * (1.0 - mask_float[None, :, :] * (1.0 - density)[:, None, None])


def apply_collisions(
    current_moments,
    collision_band,
    first_selection,
    second_selection,
    moment_weights,
    relaxation_applied,
):
    first_part = jnp.einsum(
        "js,suv->juv", first_selection, current_moments, precision=highest_degree
    )
    second_part = jnp.einsum(
        "js,suv->juv", second_selection, current_moments, precision=highest_degree
    )
    target = moment_weights[:, None, None] * first_part * second_part
    moment_mixing = jnp.einsum(
        "js,suv->juv", collision_band, current_moments, precision=highest_degree
    )
    return current_moments + collide_step * (
        moment_mixing - relaxation_applied[:, None, None] * (current_moments - target)
    )


def local(input_moments, solid_cell_mask, collision_coefficients, relaxation_rates):
    (
        axial_matrix,
        cross_matrix,
        degree_band_mask,
        first_selection,
        second_selection,
        moment_weights,
        relaxed,
        density,
        speed_bound,
    ) = operator_tables()
    collision_band = collision_coefficients * degree_band_mask
    relaxation_applied = relaxation_rates * relaxed
    length = input_moments.shape[1] * lax.axis_size("wa")
    cosine_table, sine_table = fourier_tables(length)
    wave_scale = wave_numbers(length)
    line_field = lax.all_to_all(input_moments, "wa", split_axis=2, concat_axis=1, tiled=True)
    mask_float = lax.all_to_all(
        solid_cell_mask, "wa", split_axis=1, concat_axis=0, tiled=True
    ).astype(jnp.float32)
    position_wa = lax.axis_index("wa")
    last_wa = lax.axis_size("wa") - 1
    for step_index in range(ITERS):
        line_field = axial_update(line_field, cosine_table, sine_table, axial_matrix, wave_scale)
        from_lower = shifted(line_field[:, :, -1:], "wa", 1)
        across_lower = from_behind(from_lower, "gy", 1)
        lower_line = jnp.where(position_wa == 0, across_lower, from_lower)
        from_upper = shifted(line_field[:, :, :1], "wa", -1)
        across_upper = from_behind(from_upper, "gy", -1)
        upper_line = jnp.where(position_wa == last_wa, across_upper, from_upper)
        padded = jnp.concatenate([lower_line, line_field, upper_line], axis=2)
        line_field = cross_update(
            line_field, padded[:, :, :-2], padded[:, :, 2:], cross_matrix, speed_bound
        )
        line_field = apply_walls(line_field, mask_float, density)
        line_field = apply_collisions(
            line_field,
            collision_band,
            first_selection,
            second_selection,
            moment_weights,
            relaxation_applied,
        )
    return lax.all_to_all(line_field, "wa", split_axis=1, concat_axis=2, tiled=True)


def solution(mesh):
    in_specs = (P(None, "wa", "gy"), P("wa", "gy"), P(), P())
    out_specs = P(None, "wa", "gy")
    return jax.shard_map(local, mesh=mesh, in_specs=in_specs, out_specs=out_specs, check_vma=False)
```

profile of v0, /device:TPU:0, one launch (start us, length us, event | category | flops | bytes accessed | tf_op | source)
XLA Modules:
  0.0 70.9 jit_solution(14473174839798971628)
XLA Ops:
  0.0 1.5 %copy.19 = f32[120,8,16]{0,1,2:T(8,128)} copy(f32[120,8,16]{0,2,1:T(8,128)} %param.12) | data formatting | bytes 122880 | tf_op args[0]
  1.5 7.4 %all-to-all-start = ((f32[120,8,16]{0,1,2:T(8,128)}), f32[120,8,16]{0,1,2:T(8,128)S(1)}, u32[]{:S(2)}, u32[]{:S(2)}) async-start(f32[120,8,16]{0,1,2:T(8,128)} %copy.19), calls=%async_computation | async-start | bytes 131072 | tf_op jit(solution)/shard_map/all_to_all | solution.py:217
  8.9 6.9 %all-to-all-done = f32[120,8,16]{0,1,2:T(8,128)S(1)} async-done(((f32[120,8,16]{0,1,2:T(8,128)}), f32[120,8,16]{0,1,2:T(8,128)S(1)}, u32[]{:S(2)}, u32[]{:S(2)}) %all-to-all-start) | async-done | bytes 61472 | tf_op jit(solution)/shard_map/all_to_all | solution.py:217
  15.8 0.5 fusion.59
  17.1 0.5 convolution_negate_fusion.1
  18.4 0.3 fusion.38
  18.9 0.5 fusion.92
  19.5 0.5 convolution_subtract_fusion.1
  20.1 4.4 %collective-permute-start = (f32[120,128,1]{1,0,2:T(8,128)S(1)}, f32[120,128,1]{1,0,2:T(8,128)S(1)}, u32[]{:S(2)}, u32[]{:S(2)}) collective-permute-start(f32[120,128,1]{1,0,2:T(8,128)S(1)} %multiply_bitcast_fusion.1), channel_id=1, source_target_pairs={{0,30},{2,0},{4,2},{6,4},{8,6},{10,8},{12,10},{14,12},{16,14},{18,... | collective-permute-start | bytes 184328 | tf_op jit(solution)/shard_map/ppermute | solution.py:18
  24.5 0.7 copy.20
  25.2 3.5 %all-to-all-start.1 = ((s32[8,16,1]{0,2,1:T(1,128)}), s32[8,16,1]{0,2,1:T(1,128)S(1)}, u32[]{:S(2)}, u32[]{:S(2)}) async-start(s32[8,16,1]{0,2,1:T(1,128)} %copy.20), calls=%async_computation.1 | async-start | bytes 16384 | tf_op jit(solution)/shard_map/all_to_all | solution.py:218
  28.7 0.6 copy-done.9
  29.4 3.4 %collective-permute-start.3 = (f32[120,128,1]{1,0,2:T(8,128)S(1)}, f32[120,128,1]{1,0,2:T(8,128)S(1)}, u32[]{:S(2)}, u32[]{:S(2)}) collective-permute-start(f32[120,128,1]{1,0,2:T(8,128)S(1)} %collective-permute-done.2), channel_id=1, source_target_pairs={{0,1},{2,3},{4,5},{6,7},{8,9},{10,11},{12,13},{14,15},{16,17},{18,... | collective-permute-start | bytes 184328 | tf_op jit(solution)/shard_map/ppermute | solution.py:24
  32.8 1.3 %collective-permute-start.1 = (f32[120,128,1]{1,0,2:T(8,128)S(1)}, f32[120,128,1]{1,0,2:T(8,128)S(1)}, u32[]{:S(2)}, u32[]{:S(2)}) collective-permute-start(f32[120,128,1]{1,0,2:T(8,128)S(1)} %collective-permute-done), channel_id=1, source_target_pairs={{1,0},{3,2},{5,4},{7,6},{9,8},{11,10},{13,12},{15,14},{17,16},{19,... | collective-permute-start | bytes 184328 | tf_op jit(solution)/shard_map/ppermute | solution.py:24
  34.1 0.9 %all-to-all-done.1 = s32[8,16,1]{0,2,1:T(1,128)S(1)} async-done(((s32[8,16,1]{0,2,1:T(1,128)}), s32[8,16,1]{0,2,1:T(1,128)S(1)}, u32[]{:S(2)}, u32[]{:S(2)}) %all-to-all-start.1) | async-done | bytes 544 | tf_op jit(solution)/shard_map/all_to_all | solution.py:218
  35.2 3.8 %collective-permute-done.1 = f32[120,128,1]{1,0,2:T(8,128)S(1)} collective-permute-done((f32[120,128,1]{1,0,2:T(8,128)S(1)}, f32[120,128,1]{1,0,2:T(8,128)S(1)}, u32[]{:S(2)}, u32[]{:S(2)}) %collective-permute-start.1) | collective-permute-done | bytes 61472 | tf_op jit(solution)/shard_map/ppermute | solution.py:24
  39.0 0.3 fusion.42
  39.5 0.6 copy-done.3
  40.6 0.5 convolution_negate_fusion
  41.1 0.5 fusion.90
  43.2 0.3 fusion.48
  43.7 0.5 fusion.88
  44.2 0.5 convolution_subtract_fusion
  44.8 4.4 %collective-permute-start.4 = (f32[120,128,1]{1,0,2:T(8,128)S(1)}, f32[120,128,1]{1,0,2:T(8,128)S(1)}, u32[]{:S(2)}, u32[]{:S(2)}) collective-permute-start(f32[120,128,1]{1,0,2:T(8,128)S(1)} %multiply_bitcast_fusion), channel_id=1, source_target_pairs={{0,30},{2,0},{4,2},{6,4},{8,6},{10,8},{12,10},{14,12},{16,14},{18,... | collective-permute-start | bytes 184328 | tf_op jit(solution)/shard_map/ppermute | solution.py:18
  49.3 2.0 %collective-permute-done.6 = f32[120,128,1]{1,0,2:T(8,128)S(1)} collective-permute-done((f32[120,128,1]{1,0,2:T(8,128)S(1)}, f32[120,128,1]{1,0,2:T(8,128)S(1)}, u32[]{:S(2)}, u32[]{:S(2)}) %collective-permute-start.6) | collective-permute-done | bytes 61472 | tf_op jit(solution)/shard_map/ppermute | solution.py:18
  51.2 1.6 %collective-permute-start.7 = (f32[120,128,1]{1,0,2:T(8,128)S(1)}, f32[120,128,1]{1,0,2:T(8,128)S(1)}, u32[]{:S(2)}, u32[]{:S(2)}) collective-permute-start(f32[120,128,1]{1,0,2:T(8,128)S(1)} %collective-permute-done.6), channel_id=1, source_target_pairs={{0,1},{2,3},{4,5},{6,7},{8,9},{10,11},{12,13},{14,15},{16,17},{18,... | collective-permute-start | bytes 184328 | tf_op jit(solution)/shard_map/ppermute | solution.py:24
  52.8 1.3 %collective-permute-start.5 = (f32[120,128,1]{1,0,2:T(8,128)S(1)}, f32[120,128,1]{1,0,2:T(8,128)S(1)}, u32[]{:S(2)}, u32[]{:S(2)}) collective-permute-start(f32[120,128,1]{1,0,2:T(8,128)S(1)} %collective-permute-done.4), channel_id=1, source_target_pairs={{1,0},{3,2},{5,4},{7,6},{9,8},{11,10},{13,12},{15,14},{17,16},{19,... | collective-permute-start | bytes 184328 | tf_op jit(solution)/shard_map/ppermute | solution.py:24
  54.1 0.5 collective-permute-done.7
  54.7 4.3 %collective-permute-done.5 = f32[120,128,1]{1,0,2:T(8,128)S(1)} collective-permute-done((f32[120,128,1]{1,0,2:T(8,128)S(1)}, f32[120,128,1]{1,0,2:T(8,128)S(1)}, u32[]{:S(2)}, u32[]{:S(2)}) %collective-permute-start.5) | collective-permute-done | bytes 61472 | tf_op jit(solution)/shard_map/ppermute | solution.py:24
  58.9 0.3 fusion.52
  60.1 10.2 %all_to_all.46 = f32[120,128,1]{0,2,1:T(1,128)S(1)} all-to-all(f32[120,128,1]{0,2,1:T(1,128)S(1)} %copy.21), channel_id=1, replica_groups=mesh['wa'=16,'gy'=2] {'wa'}, dimensions={1} | all-to-all | bytes 122880 | tf_op jit(solution)/shard_map/all_to_all | solution.py:244
  70.3 0.6 copy.22
  (54 shorter events, 5.5 us)
Async XLA Ops:
  1.5 14.3 %all-to-all-start = ((f32[120,8,16]{0,1,2:T(8,128)}), f32[120,8,16]{0,1,2:T(8,128)S(1)}, u32[]{:S(2)}, u32[]{:S(2)}) async-start(f32[120,8,16]{0,1,2:T(8,128)} %copy.19), calls=%async_computation | async-start | bytes 131072 | tf_op jit(solution)/shard_map/all_to_all | solution.py:217
  8.9 7.4 %copy-start = (f32[120,120]{1,0:T(8,128)S(1)}, f32[120,120]{1,0:T(8,128)}, u32[]{:S(2)}) copy-start(f32[120,120]{1,0:T(8,128)} %constant.82.clone) | copy-start | bytes 172804
  19.5 5.1 %copy-start.6 = (s32[8,16]{1,0:T(8,128)S(1)}, s32[8,16]{1,0:T(8,128)}, u32[]{:S(2)}) copy-start(s32[8,16]{1,0:T(8,128)} %param.13) | copy-start | bytes 1540
  20.0 9.4 %copy-start.4 = (f32[120,120]{1,0:T(8,128)S(1)}, f32[120,120]{1,0:T(8,128)}, u32[]{:S(2)}) copy-start(f32[120,120]{1,0:T(8,128)} %param.14) | copy-start | bytes 172804
  20.0 9.4 %copy-start.5 = (f32[120,120]{1,0:T(8,128)S(1)}, f32[120,120]{1,0:T(8,128)}, u32[]{:S(2)}) copy-start(f32[120,120]{1,0:T(8,128)} %constant.84.clone) | copy-start | bytes 172804
  20.0 9.4 %collective-permute-start.2 = (f32[120,128,1]{1,0,2:T(8,128)S(1)}, f32[120,128,1]{1,0,2:T(8,128)S(1)}, u32[]{:S(2)}, u32[]{:S(2)}) collective-permute-start(f32[120,128,1]{1,0,2:T(8,128)S(1)} %multiply_bitcast_fusion.1), channel_id=1, source_target_pairs={{0,2},{2,4},{4,6},{6,8},{8,10},{10,12},{12,14},{14,16},{16,18},{18... | collective-permute-start | bytes 184328 | tf_op jit(solution)/shard_map/ppermute | solution.py:18
  20.1 12.7 %collective-permute-start = (f32[120,128,1]{1,0,2:T(8,128)S(1)}, f32[120,128,1]{1,0,2:T(8,128)S(1)}, u32[]{:S(2)}, u32[]{:S(2)}) collective-permute-start(f32[120,128,1]{1,0,2:T(8,128)S(1)} %multiply_bitcast_fusion.1), channel_id=1, source_target_pairs={{0,30},{2,0},{4,2},{6,4},{8,6},{10,8},{12,10},{14,12},{16,14},{18,... | collective-permute-start | bytes 184328 | tf_op jit(solution)/shard_map/ppermute | solution.py:18
  25.2 9.8 %all-to-all-start.1 = ((s32[8,16,1]{0,2,1:T(1,128)}), s32[8,16,1]{0,2,1:T(1,128)S(1)}, u32[]{:S(2)}, u32[]{:S(2)}) async-start(s32[8,16,1]{0,2,1:T(1,128)} %copy.20), calls=%async_computation.1 | async-start | bytes 16384 | tf_op jit(solution)/shard_map/all_to_all | solution.py:218
  28.7 0.7 copy-start.9
  28.7 0.7 copy-start.10
  29.4 9.6 %copy-start.2 = (f32[120,120]{1,0:T(8,128)S(1)}, f32[120,120]{1,0:T(8,128)}, u32[]{:S(2)}) copy-start(f32[120,120]{1,0:T(8,128)} %constant.83.clone) | copy-start | bytes 172804
  29.4 5.7 %collective-permute-start.3 = (f32[120,128,1]{1,0,2:T(8,128)S(1)}, f32[120,128,1]{1,0,2:T(8,128)S(1)}, u32[]{:S(2)}, u32[]{:S(2)}) collective-permute-start(f32[120,128,1]{1,0,2:T(8,128)S(1)} %collective-permute-done.2), channel_id=1, source_target_pairs={{0,1},{2,3},{4,5},{6,7},{8,9},{10,11},{12,13},{14,15},{16,17},{18,... | collective-permute-start | bytes 184328 | tf_op jit(solution)/shard_map/ppermute | solution.py:24
  32.8 6.1 %collective-permute-start.1 = (f32[120,128,1]{1,0,2:T(8,128)S(1)}, f32[120,128,1]{1,0,2:T(8,128)S(1)}, u32[]{:S(2)}, u32[]{:S(2)}) collective-permute-start(f32[120,128,1]{1,0,2:T(8,128)S(1)} %collective-permute-done), channel_id=1, source_target_pairs={{1,0},{3,2},{5,4},{7,6},{9,8},{11,10},{13,12},{15,14},{17,16},{19,... | collective-permute-start | bytes 184328 | tf_op jit(solution)/shard_map/ppermute | solution.py:24
  35.0 3.9 %copy-start.8 = (f32[120]{0:T(128)S(1)}, f32[120]{0:T(128)}, u32[]{:S(2)}) copy-start(f32[120]{0:T(128)} %constant.93) | copy-start | bytes 1444
  35.1 4.1 %copy-start.1 = (f32[120,120]{1,0:T(8,128)S(1)}, f32[120,120]{1,0:T(8,128)}, u32[]{:S(2)}) copy-start(f32[120,120]{1,0:T(8,128)} %constant.85.clone) | copy-start | bytes 172804
  35.2 4.1 %copy-start.7 = (f32[120]{0:T(128)S(1)}, f32[120]{0:T(128)}, u32[]{:S(2)}) copy-start(f32[120]{0:T(128)} %constant.87.clone) | copy-start | bytes 1444
  39.3 0.8 %copy-start.3 = (f32[120,120]{1,0:T(8,128)S(1)}, f32[120,120]{1,0:T(8,128)}, u32[]{:S(2)}) copy-start(f32[120,120]{1,0:T(8,128)} %constant.86.clone) | copy-start | bytes 172804
  44.8 6.5 %collective-permute-start.6 = (f32[120,128,1]{1,0,2:T(8,128)S(1)}, f32[120,128,1]{1,0,2:T(8,128)S(1)}, u32[]{:S(2)}, u32[]{:S(2)}) collective-permute-start(f32[120,128,1]{1,0,2:T(8,128)S(1)} %multiply_bitcast_fusion), channel_id=1, source_target_pairs={{0,2},{2,4},{4,6},{6,8},{8,10},{10,12},{12,14},{14,16},{16,18},{18... | collective-permute-start | bytes 184328 | tf_op jit(solution)/shard_map/ppermute | solution.py:18
  44.8 8.0 %collective-permute-start.4 = (f32[120,128,1]{1,0,2:T(8,128)S(1)}, f32[120,128,1]{1,0,2:T(8,128)S(1)}, u32[]{:S(2)}, u32[]{:S(2)}) collective-permute-start(f32[120,128,1]{1,0,2:T(8,128)S(1)} %multiply_bitcast_fusion), channel_id=1, source_target_pairs={{0,30},{2,0},{4,2},{6,4},{8,6},{10,8},{12,10},{14,12},{16,14},{18,... | collective-permute-start | bytes 184328 | tf_op jit(solution)/shard_map/ppermute | solution.py:18
  51.2 3.4 %collective-permute-start.7 = (f32[120,128,1]{1,0,2:T(8,128)S(1)}, f32[120,128,1]{1,0,2:T(8,128)S(1)}, u32[]{:S(2)}, u32[]{:S(2)}) collective-permute-start(f32[120,128,1]{1,0,2:T(8,128)S(1)} %collective-permute-done.6), channel_id=1, source_target_pairs={{0,1},{2,3},{4,5},{6,7},{8,9},{10,11},{12,13},{14,15},{16,17},{18,... | collective-permute-start | bytes 184328 | tf_op jit(solution)/shard_map/ppermute | solution.py:24
  52.8 6.1 %collective-permute-start.5 = (f32[120,128,1]{1,0,2:T(8,128)S(1)}, f32[120,128,1]{1,0,2:T(8,128)S(1)}, u32[]{:S(2)}, u32[]{:S(2)}) collective-permute-start(f32[120,128,1]{1,0,2:T(8,128)S(1)} %collective-permute-done.4), channel_id=1, source_target_pairs={{1,0},{3,2},{5,4},{7,6},{9,8},{11,10},{13,12},{15,14},{17,16},{19,... | collective-permute-start | bytes 184328 | tf_op jit(solution)/shard_map/ppermute | solution.py:24
where the time goes:
time: 71.4 us; the launch traced here: 70.9 us
  starting transfers between devices  27.4 us (38%)
  waiting for transfers between devices  18.3 us (26%)
  matrix products  10.2 us (14%)
  blocking collectives  10.2 us (14%)
  local copies, waits for them, and re-layouts  4.25 us (6%)
    all_to_all x1, blocking collectives, local(): lax.all_to_all(line_field, 'wa', split_axis=1, concat_axis=2, tiled=True)  10.2 us
    ppermute x4, starting transfers between devices, shifted(): lax.ppermute(value, axis, [(i, (i + by) % count) for i in range(count)])  8.97 us
    ppermute x4, waiting for transfers between devices, from_behind(): return lax.ppermute(value, axis, pairs)  8.6 us
    ppermute x4, starting transfers between devices, from_behind(): return lax.ppermute(value, axis, pairs)  7.55 us
    all_to_all x1, starting transfers between devices, local(): lax.all_to_all(input_moments, 'wa', split_axis=2, concat_axis=1, tiled=True)  7.41 us
    all_to_all x1, waiting for transfers between devices, local(): lax.all_to_all(input_moments, 'wa', split_axis=2, concat_axis=1, tiled=True)  6.87 us
    all_to_all x1, starting transfers between devices, local(): lax.all_to_all(solid_cell_mask, 'wa', split_axis=1, concat_axis=0, tiled=...  3.47 us
    unnamed x23, local copies, waits for them, and re-layouts  2.77 us
  transfers between devices with their start and end apart: 10, of which 6 were waited for; matrix products, arithmetic and copies ran while one was open for 1% of the time, Pallas kernels for 0%

commit v1 on v0

--- a/solution.py
+++ b/solution.py
@@ -1,3 +1,4 @@
+import functools
 import math
 import jax
 import jax.numpy as jnp
@@ -11,6 +12,17 @@
 axial_step = 0.2
 cross_step = 0.2
 collide_step = 0.5
+
+
+def spans_follow(m, shard_axis):
+    b_now = lax.psum(1, shard_axis)
+    block_out = jnp.split(m, b_now, axis=2)
+    found_now = jnp.stack(block_out)
+    heard = lax.all_to_all(found_now, shard_axis, 0, 0)
+    return jnp.concatenate(heard, axis=1)
+
+
+spread_group = functools.partial(spans_follow, shard_axis="wa")
 
 
 def shifted(value, axis, by):
@@ -214,7 +226,7 @@
     length = input_moments.shape[1] * lax.axis_size("wa")
     cosine_table, sine_table = fourier_tables(length)
     wave_scale = wave_numbers(length)
-    line_field = lax.all_to_all(input_moments, "wa", split_axis=2, concat_axis=1, tiled=True)
+    line_field = spread_group(input_moments)
     mask_float = lax.all_to_all(
         solid_cell_mask, "wa", split_axis=1, concat_axis=0, tiled=True
     ).astype(jnp.float32)

time: 71.4 us -> 80.7 us (1.13)
  local copies, waits for them, and re-layouts: 4.25 us -> 13.5 us
    unnamed x23 -> x37, local copies, waits for them, and re-layouts: 2.77 us -> 10.2 us
    split x0 -> x1, local copies, waits for them, and re-layouts: none -> 1.29 us  [spans_follow(): block_out = jnp.split(m, b_now, axis=2)]
where the time goes in v1:
time: 80.7 us; the launch traced here: 80.2 us
  starting transfers between devices  27.4 us (34%)
  waiting for transfers between devices  18.3 us (23%)
  local copies, waits for them, and re-layouts  13.5 us (17%)
  matrix products  10.2 us (13%)
  blocking collectives  10.2 us (13%)
    unnamed x37, local copies, waits for them, and re-layouts  10.2 us
    all_to_all x1, blocking collectives, local(): lax.all_to_all(line_field, 'wa', split_axis=1, concat_axis=2, tiled=True)  10.2 us
    ppermute x4, starting transfers between devices, shifted(): lax.ppermute(value, axis, [(i, (i + by) % count) for i in range(count)])  8.97 us
    ppermute x4, waiting for transfers between devices, from_behind(): return lax.ppermute(value, axis, pairs)  8.59 us
    ppermute x4, starting transfers between devices, from_behind(): return lax.ppermute(value, axis, pairs)  7.55 us
    all_to_all x1, starting transfers between devices, spans_follow(): heard = lax.all_to_all(found_now, shard_axis, 0, 0)  7.41 us
    all_to_all x1, waiting for transfers between devices, spans_follow(): heard = lax.all_to_all(found_now, shard_axis, 0, 0)  6.87 us
    all_to_all x1, starting transfers between devices, local(): lax.all_to_all(solid_cell_mask, 'wa', split_axis=1, concat_axis=0, tiled=...  3.47 us
  transfers between devices with their start and end apart: 10, of which 6 were waited for; matrix products, arithmetic and copies ran while one was open for 1% of the time, Pallas kernels for 0%

profile of v1, /device:TPU:0, one launch (start us, length us, event | category | flops | bytes accessed | tf_op | source)
XLA Modules:
  0.0 80.2 jit_solution(3723301391047521068)
XLA Ops:
  0.0 1.3 %fusion.137 = (f32[120,8,1]{0,2,1:T(1,128)S(1)}, f32[120,8,1]{0,2,1:T(1,128)S(1)}, f32[120,8,1]{0,2,1:T(1,128)S(1)}, f32[120,8,1]{0,2,1:T(1,128)S(1)}, f32[120,8...) fusion(f32[120,8,16]{0,2,1:T(8,128)} %param.12), kind=kLoop, calls=%fused_computation.195 | loop fusion | bytes 122880 | tf_op jit(solution)/shard_map/split | solution.py:19
  1.3 0.6 constant_dynamic-update-slice_fusion.15
  1.9 0.6 constant_dynamic-update-slice_fusion.14
  2.5 0.6 constant_dynamic-update-slice_fusion.13
  3.1 0.6 constant_dynamic-update-slice_fusion.12
  3.7 0.6 constant_dynamic-update-slice_fusion.11
  4.3 0.6 constant_dynamic-update-slice_fusion.10
  4.9 0.6 constant_dynamic-update-slice_fusion.9
  6.0 0.6 constant_dynamic-update-slice_fusion.7
  6.6 0.6 constant_dynamic-update-slice_fusion.6
  7.2 0.6 constant_dynamic-update-slice_fusion.5
  7.8 0.6 constant_dynamic-update-slice_fusion.4
  9.0 0.6 constant_dynamic-update-slice_fusion.2
  9.6 0.6 constant_dynamic-update-slice_fusion.1
  10.2 0.6 constant_dynamic-update-slice_fusion
  10.8 7.4 %all-to-all-start = ((f32[16,120,8,1]{1,2,3,0:T(8,128)}), f32[16,120,8,1]{1,2,3,0:T(8,128)S(1)}, u32[]{:S(2)}, u32[]{:S(2)}) async-start(f32[16,120,8,1]{1,2,3,0:T(8,128)} %constant_dynamic-update-slice_fusion), calls=%async_computation | async-start | bytes 131072 | tf_op jit(solution)/shard_map/all_to_all | solution.py:21
  18.2 6.9 %all-to-all-done = f32[16,120,8,1]{1,2,3,0:T(8,128)S(1)} async-done(((f32[16,120,8,1]{1,2,3,0:T(8,128)}), f32[16,120,8,1]{1,2,3,0:T(8,128)S(1)}, u32[]{:S(2)}, u32[]{:S(2)}) %all-to-all-start) | async-done | bytes 61472 | tf_op jit(solution)/shard_map/all_to_all | solution.py:21
  29.4 4.4 %collective-permute-start = (f32[120,128,1]{1,0,2:T(8,128)S(1)}, f32[120,128,1]{1,0,2:T(8,128)S(1)}, u32[]{:S(2)}, u32[]{:S(2)}) collective-permute-start(f32[120,128,1]{1,0,2:T(8,128)S(1)} %multiply_bitcast_fusion.1), channel_id=1, source_target_pairs={{0,30},{2,0},{4,2},{6,4},{8,6},{10,8},{12,10},{14,12},{16,14},{18,... | collective-permute-start | bytes 184328 | tf_op jit(solution)/shard_map/ppermute | solution.py:30
  33.8 0.7 copy.63
  34.5 3.5 %all-to-all-start.1 = ((s32[8,16,1]{0,2,1:T(1,128)}), s32[8,16,1]{0,2,1:T(1,128)S(1)}, u32[]{:S(2)}, u32[]{:S(2)}) async-start(s32[8,16,1]{0,2,1:T(1,128)} %copy.63), calls=%async_computation.1 | async-start | bytes 16384 | tf_op jit(solution)/shard_map/all_to_all | solution.py:230
  38.0 0.6 copy-done.9
  38.7 3.4 %collective-permute-start.3 = (f32[120,128,1]{1,0,2:T(8,128)S(1)}, f32[120,128,1]{1,0,2:T(8,128)S(1)}, u32[]{:S(2)}, u32[]{:S(2)}) collective-permute-start(f32[120,128,1]{1,0,2:T(8,128)S(1)} %collective-permute-done.2), channel_id=1, source_target_pairs={{0,1},{2,3},{4,5},{6,7},{8,9},{10,11},{12,13},{14,15},{16,17},{18,... | collective-permute-start | bytes 184328 | tf_op jit(solution)/shard_map/ppermute | solution.py:36
  42.1 1.3 %collective-permute-start.1 = (f32[120,128,1]{1,0,2:T(8,128)S(1)}, f32[120,128,1]{1,0,2:T(8,128)S(1)}, u32[]{:S(2)}, u32[]{:S(2)}) collective-permute-start(f32[120,128,1]{1,0,2:T(8,128)S(1)} %collective-permute-done), channel_id=1, source_target_pairs={{1,0},{3,2},{5,4},{7,6},{9,8},{11,10},{13,12},{15,14},{17,16},{19,... | collective-permute-start | bytes 184328 | tf_op jit(solution)/shard_map/ppermute | solution.py:36
  43.4 0.9 %all-to-all-done.1 = s32[8,16,1]{0,2,1:T(1,128)S(1)} async-done(((s32[8,16,1]{0,2,1:T(1,128)}), s32[8,16,1]{0,2,1:T(1,128)S(1)}, u32[]{:S(2)}, u32[]{:S(2)}) %all-to-all-start.1) | async-done | bytes 544 | tf_op jit(solution)/shard_map/all_to_all | solution.py:230
  44.5 3.8 %collective-permute-done.1 = f32[120,128,1]{1,0,2:T(8,128)S(1)} collective-permute-done((f32[120,128,1]{1,0,2:T(8,128)S(1)}, f32[120,128,1]{1,0,2:T(8,128)S(1)}, u32[]{:S(2)}, u32[]{:S(2)}) %collective-permute-start.1) | collective-permute-done | bytes 61472 | tf_op jit(solution)/shard_map/ppermute | solution.py:36
  54.2 4.4 %collective-permute-start.4 = (f32[120,128,1]{1,0,2:T(8,128)S(1)}, f32[120,128,1]{1,0,2:T(8,128)S(1)}, u32[]{:S(2)}, u32[]{:S(2)}) collective-permute-start(f32[120,128,1]{1,0,2:T(8,128)S(1)} %multiply_bitcast_fusion), channel_id=1, source_target_pairs={{0,30},{2,0},{4,2},{6,4},{8,6},{10,8},{12,10},{14,12},{16,14},{18,... | collective-permute-start | bytes 184328 | tf_op jit(solution)/shard_map/ppermute | solution.py:30
  58.6 2.0 %collective-permute-done.6 = f32[120,128,1]{1,0,2:T(8,128)S(1)} collective-permute-done((f32[120,128,1]{1,0,2:T(8,128)S(1)}, f32[120,128,1]{1,0,2:T(8,128)S(1)}, u32[]{:S(2)}, u32[]{:S(2)}) %collective-permute-start.6) | collective-permute-done | bytes 61472 | tf_op jit(solution)/shard_map/ppermute | solution.py:30
  60.5 1.6 %collective-permute-start.7 = (f32[120,128,1]{1,0,2:T(8,128)S(1)}, f32[120,128,1]{1,0,2:T(8,128)S(1)}, u32[]{:S(2)}, u32[]{:S(2)}) collective-permute-start(f32[120,128,1]{1,0,2:T(8,128)S(1)} %collective-permute-done.6), channel_id=1, source_target_pairs={{0,1},{2,3},{4,5},{6,7},{8,9},{10,11},{12,13},{14,15},{16,17},{18,... | collective-permute-start | bytes 184328 | tf_op jit(solution)/shard_map/ppermute | solution.py:36
  62.1 1.3 %collective-permute-start.5 = (f32[120,128,1]{1,0,2:T(8,128)S(1)}, f32[120,128,1]{1,0,2:T(8,128)S(1)}, u32[]{:S(2)}, u32[]{:S(2)}) collective-permute-start(f32[120,128,1]{1,0,2:T(8,128)S(1)} %collective-permute-done.4), channel_id=1, source_target_pairs={{1,0},{3,2},{5,4},{7,6},{9,8},{11,10},{13,12},{15,14},{17,16},{19,... | collective-permute-start | bytes 184328 | tf_op jit(solution)/shard_map/ppermute | solution.py:36
  64.0 4.3 %collective-permute-done.5 = f32[120,128,1]{1,0,2:T(8,128)S(1)} collective-permute-done((f32[120,128,1]{1,0,2:T(8,128)S(1)}, f32[120,128,1]{1,0,2:T(8,128)S(1)}, u32[]{:S(2)}, u32[]{:S(2)}) %collective-permute-start.5) | collective-permute-done | bytes 61472 | tf_op jit(solution)/shard_map/ppermute | solution.py:36
  69.4 10.2 %all_to_all.36 = f32[120,128,1]{0,2,1:T(1,128)S(1)} all-to-all(f32[120,128,1]{0,2,1:T(1,128)S(1)} %copy.64), channel_id=1, replica_groups=mesh['wa'=16,'gy'=2] {'wa'}, dimensions={1} | all-to-all | bytes 122880 | tf_op jit(solution)/shard_map/all_to_all | solution.py:256
  79.6 0.6 copy.65
  (70 shorter events, 13.0 us)
Async XLA Ops:
  10.8 14.3 %all-to-all-start = ((f32[16,120,8,1]{1,2,3,0:T(8,128)}), f32[16,120,8,1]{1,2,3,0:T(8,128)S(1)}, u32[]{:S(2)}, u32[]{:S(2)}) async-start(f32[16,120,8,1]{1,2,3,0:T(8,128)} %constant_dynamic-update-slice_fusion), calls=%async_computation | async-start | bytes 131072 | tf_op jit(solution)/shard_map/all_to_all | solution.py:21
  18.2 7.4 %copy-start = (f32[120,120]{1,0:T(8,128)S(1)}, f32[120,120]{1,0:T(8,128)}, u32[]{:S(2)}) copy-start(f32[120,120]{1,0:T(8,128)} %constant.82.clone) | copy-start | bytes 172804
  28.8 5.1 %copy-start.6 = (s32[8,16]{1,0:T(8,128)S(1)}, s32[8,16]{1,0:T(8,128)}, u32[]{:S(2)}) copy-start(s32[8,16]{1,0:T(8,128)} %param.13) | copy-start | bytes 1540
  29.3 9.4 %copy-start.4 = (f32[120,120]{1,0:T(8,128)S(1)}, f32[120,120]{1,0:T(8,128)}, u32[]{:S(2)}) copy-start(f32[120,120]{1,0:T(8,128)} %param.14) | copy-start | bytes 172804
  29.3 9.4 %copy-start.5 = (f32[120,120]{1,0:T(8,128)S(1)}, f32[120,120]{1,0:T(8,128)}, u32[]{:S(2)}) copy-start(f32[120,120]{1,0:T(8,128)} %constant.84.clone) | copy-start | bytes 172804
  29.3 9.4 %collective-permute-start.2 = (f32[120,128,1]{1,0,2:T(8,128)S(1)}, f32[120,128,1]{1,0,2:T(8,128)S(1)}, u32[]{:S(2)}, u32[]{:S(2)}) collective-permute-start(f32[120,128,1]{1,0,2:T(8,128)S(1)} %multiply_bitcast_fusion.1), channel_id=1, source_target_pairs={{0,2},{2,4},{4,6},{6,8},{8,10},{10,12},{12,14},{14,16},{16,18},{18... | collective-permute-start | bytes 184328 | tf_op jit(solution)/shard_map/ppermute | solution.py:30
  29.4 12.7 %collective-permute-start = (f32[120,128,1]{1,0,2:T(8,128)S(1)}, f32[120,128,1]{1,0,2:T(8,128)S(1)}, u32[]{:S(2)}, u32[]{:S(2)}) collective-permute-start(f32[120,128,1]{1,0,2:T(8,128)S(1)} %multiply_bitcast_fusion.1), channel_id=1, source_target_pairs={{0,30},{2,0},{4,2},{6,4},{8,6},{10,8},{12,10},{14,12},{16,14},{18,... | collective-permute-start | bytes 184328 | tf_op jit(solution)/shard_map/ppermute | solution.py:30
  34.5 9.8 %all-to-all-start.1 = ((s32[8,16,1]{0,2,1:T(1,128)}), s32[8,16,1]{0,2,1:T(1,128)S(1)}, u32[]{:S(2)}, u32[]{:S(2)}) async-start(s32[8,16,1]{0,2,1:T(1,128)} %copy.63), calls=%async_computation.1 | async-start | bytes 16384 | tf_op jit(solution)/shard_map/all_to_all | solution.py:230
  38.0 0.7 copy-start.9
  38.0 0.7 copy-start.10
  38.7 9.6 %copy-start.2 = (f32[120,120]{1,0:T(8,128)S(1)}, f32[120,120]{1,0:T(8,128)}, u32[]{:S(2)}) copy-start(f32[120,120]{1,0:T(8,128)} %constant.83.clone) | copy-start | bytes 172804
  38.7 5.7 %collective-permute-start.3 = (f32[120,128,1]{1,0,2:T(8,128)S(1)}, f32[120,128,1]{1,0,2:T(8,128)S(1)}, u32[]{:S(2)}, u32[]{:S(2)}) collective-permute-start(f32[120,128,1]{1,0,2:T(8,128)S(1)} %collective-permute-done.2), channel_id=1, source_target_pairs={{0,1},{2,3},{4,5},{6,7},{8,9},{10,11},{12,13},{14,15},{16,17},{18,... | collective-permute-start | bytes 184328 | tf_op jit(solution)/shard_map/ppermute | solution.py:36
  42.1 6.1 %collective-permute-start.1 = (f32[120,128,1]{1,0,2:T(8,128)S(1)}, f32[120,128,1]{1,0,2:T(8,128)S(1)}, u32[]{:S(2)}, u32[]{:S(2)}) collective-permute-start(f32[120,128,1]{1,0,2:T(8,128)S(1)} %collective-permute-done), channel_id=1, source_target_pairs={{1,0},{3,2},{5,4},{7,6},{9,8},{11,10},{13,12},{15,14},{17,16},{19,... | collective-permute-start | bytes 184328 | tf_op jit(solution)/shard_map/ppermute | solution.py:36
  44.3 3.9 %copy-start.8 = (f32[120]{0:T(128)S(1)}, f32[120]{0:T(128)}, u32[]{:S(2)}) copy-start(f32[120]{0:T(128)} %constant.93) | copy-start | bytes 1444
  44.4 4.1 %copy-start.1 = (f32[120,120]{1,0:T(8,128)S(1)}, f32[120,120]{1,0:T(8,128)}, u32[]{:S(2)}) copy-start(f32[120,120]{1,0:T(8,128)} %constant.85.clone) | copy-start | bytes 172804
  44.5 4.1 %copy-start.7 = (f32[120]{0:T(128)S(1)}, f32[120]{0:T(128)}, u32[]{:S(2)}) copy-start(f32[120]{0:T(128)} %constant.87.clone) | copy-start | bytes 1444
  48.6 0.8 %copy-start.3 = (f32[120,120]{1,0:T(8,128)S(1)}, f32[120,120]{1,0:T(8,128)}, u32[]{:S(2)}) copy-start(f32[120,120]{1,0:T(8,128)} %constant.86.clone) | copy-start | bytes 172804
  54.1 6.4 %collective-permute-start.6 = (f32[120,128,1]{1,0,2:T(8,128)S(1)}, f32[120,128,1]{1,0,2:T(8,128)S(1)}, u32[]{:S(2)}, u32[]{:S(2)}) collective-permute-start(f32[120,128,1]{1,0,2:T(8,128)S(1)} %multiply_bitcast_fusion), channel_id=1, source_target_pairs={{0,2},{2,4},{4,6},{6,8},{8,10},{10,12},{12,14},{14,16},{16,18},{18... | collective-permute-start | bytes 184328 | tf_op jit(solution)/shard_map/ppermute | solution.py:30
  54.2 8.0 %collective-permute-start.4 = (f32[120,128,1]{1,0,2:T(8,128)S(1)}, f32[120,128,1]{1,0,2:T(8,128)S(1)}, u32[]{:S(2)}, u32[]{:S(2)}) collective-permute-start(f32[120,128,1]{1,0,2:T(8,128)S(1)} %multiply_bitcast_fusion), channel_id=1, source_target_pairs={{0,30},{2,0},{4,2},{6,4},{8,6},{10,8},{12,10},{14,12},{16,14},{18,... | collective-permute-start | bytes 184328 | tf_op jit(solution)/shard_map/ppermute | solution.py:30
  60.5 3.4 %collective-permute-start.7 = (f32[120,128,1]{1,0,2:T(8,128)S(1)}, f32[120,128,1]{1,0,2:T(8,128)S(1)}, u32[]{:S(2)}, u32[]{:S(2)}) collective-permute-start(f32[120,128,1]{1,0,2:T(8,128)S(1)} %collective-permute-done.6), channel_id=1, source_target_pairs={{0,1},{2,3},{4,5},{6,7},{8,9},{10,11},{12,13},{14,15},{16,17},{18,... | collective-permute-start | bytes 184328 | tf_op jit(solution)/shard_map/ppermute | solution.py:36
  62.1 6.1 %collective-permute-start.5 = (f32[120,128,1]{1,0,2:T(8,128)S(1)}, f32[120,128,1]{1,0,2:T(8,128)S(1)}, u32[]{:S(2)}, u32[]{:S(2)}) collective-permute-start(f32[120,128,1]{1,0,2:T(8,128)S(1)} %collective-permute-done.4), channel_id=1, source_target_pairs={{1,0},{3,2},{5,4},{7,6},{9,8},{11,10},{13,12},{15,14},{17,16},{19,... | collective-permute-start | bytes 184328 | tf_op jit(solution)/shard_map/ppermute | solution.py:36
